TPU v7x, 32 devices: a whole 2x2x4 slice. The times are simulated.
32 devices in a mesh: trow: 4 (over y, core), tcol: 8 (over z, x).
Axes of the slice: x: 2, y: 2, z: 4, core: 2. Of those that a mesh axis runs over, the one named last changes fastest.
Arguments:
- response: bfloat16 [4096, 16384], P('trow', 'tcol'), may hold values from -0.046875 to 0.046875
- test_matrix: bfloat16 [1024, 192], P(('trow', 'tcol')), may hold values from -6 to 6
- slopes: bfloat16 [16384, 256], P('tcol', 'trow'), may hold values from -6 to 6
- ranks: int32 [4, 16], P('trow', 'tcol'), may hold values from 16 to 192, as said below
Outputs:
- commands: float32 [4096, 256], P(('trow', 'tcol'))
Inputs may be any that keep to these rules, and one draw needn't show every extreme that they name: ranks of tiles near the diagonal tend to be higher, and every tile's sketch has full column rank and is well conditioned.
All inputs are finite; a program needn't handle non-finite values.
Results may differ from a plain program's by a relative error of at most 0.014.
Values may be sent and summed in bfloat16 or wider, within the bound.
A program may use at most 64 MiB of HBM per device.

v0:
```python
import jax
import jax.numpy as jnp
from jax import lax
from jax.sharding import PartitionSpec as P


def fetch_frames(slopes):
    return lax.all_gather(slopes, "trow", axis=1, tiled=True)


def on_device(response, test_matrix, slopes, ranks):
    highest = lax.Precision.HIGHEST
    tile_rows = ranks.shape[0]
    tile_cols = ranks.shape[1]
    width = response.shape[0] // tile_rows
    sketch_width = test_matrix.shape[1]
    tiles = response.reshape(tile_rows, width, tile_cols, width)
    row_block = lax.all_gather(test_matrix, "tcol", axis=0, tiled=True)
    sketch = jnp.einsum(
        "rick,kj->rcij",
        tiles,
        lax.all_gather(row_block, "trow", axis=0, tiled=True),
        preferred_element_type=jnp.float32,
    )
    gram = jnp.einsum("rcik,rcil->rckl", sketch, sketch, precision=highest)
    chol = jnp.linalg.cholesky(gram)
    basis = jax.scipy.linalg.solve_triangular(chol, jnp.swapaxes(sketch, 2, 3), lower=True)
    slots = jnp.arange(sketch_width, dtype=jnp.int32)
    keep = (slots[None, None, :] < ranks[:, :, None]).astype(jnp.float32)
    basis = (basis * keep[:, :, :, None]).astype(jnp.bfloat16)
    factor = jnp.einsum("rcsi,ricj->rcsj", basis, tiles, preferred_element_type=jnp.float32).astype(
        jnp.bfloat16
    )
    frames = fetch_frames(slopes)
    frame_count = frames.shape[1]
    frame_tiles = frames.reshape(tile_cols, width, frame_count)
    coeff = jnp.einsum(
        "rcsj,cjf->rcsf", factor, frame_tiles, preferred_element_type=jnp.float32
    ).astype(jnp.bfloat16)
    share_rows = tile_rows * width // lax.axis_size("tcol")
    summed = jnp.einsum("rcsi,rcsf->rif", basis, coeff, preferred_element_type=jnp.float32)
    summed_all = lax.psum(
        summed.reshape(tile_rows * width, frame_count).astype(jnp.bfloat16), "tcol"
    ).astype(jnp.float32)
    result = lax.dynamic_slice_in_dim(
        summed_all, lax.axis_index("tcol") * share_rows, share_rows, 0
    )
    return result


def solution(mesh):
    return jax.shard_map(
        on_device,
        mesh=mesh,
        in_specs=(
            P("trow", "tcol"),
            P(("trow", "tcol"), None),
            P("tcol", "trow"),
            P("trow", "tcol"),
        ),
        out_specs=P(("trow", "tcol"), None),
        check_vma=False,
    )
```

profile of v0, /device:TPU:0, one launch (start us, length us, event | category | flops | bytes accessed | tf_op | source)
XLA Modules:
  0.0 238.7 jit_solution(7302587469162838817)
XLA Ops:
  6.5 0.0 all-gather.2.cloned.1.call-start
  6.5 0.7 all-gather.2.cloned.1.call-update
  7.3 0.0 all-reduce.5.cloned.1.call-start
  7.4 32.5 %all_gather.9 = bf16[256,192]{1,0:T(8,128)(2,1)S(1)} all-gather(bf16[32,192]{1,0:T(8,128)(2,1)} %param.5), channel_id=1, replica_groups=mesh['trow'=4,'tcol'=8] {'tcol'}, dimensions={0}, use_global_device_ids=true | all-gather | bytes 110592 | tf_op jit(solution)/shard_map/all_gather | solution.py:18
  39.9 0.1 copy.21
  40.1 6.5 %all_gather.10 = bf16[1024,192]{0,1:T(8,128)(2,1)S(1)} all-gather(bf16[256,192]{0,1:T(8,128)(2,1)S(1)} %copy.21), channel_id=1, replica_groups=mesh['trow'=4,'tcol'=8] {'trow'}, dimensions={0}, use_global_device_ids=true | all-gather | bytes 491520 | tf_op jit(solution)/shard_map/all_gather | solution.py:22
  46.5 3.7 %fusion.2 = f32[192,1024,2]{1,0,2:T(8,128)S(1)} fusion(bf16[128,2,8,1024]{3,2,1,0:T(8,128)(2,1)} %bitcast.77, bf16[1024,192]{0,1:T(8,128)(2,1)S(1)} %all_gather.10), kind=kOutput, calls=%fused_computation.2 | convolution fusion | flops 805306368 | bytes 6160384 | tf_op jit(solution)/shard_map/rick,kj->rcij/dot_general | solution.py:19
  50.3 1.7 fusion.7
  51.9 0.2 copy.24
  52.1 0.1 fusion.16
  52.2 23.6 %custom-call.17 = f32[1,2,128,128]{3,2,1,0:T(8,128)S(1)} custom-call(f32[1,2,128,128]{3,2,1,0:T(8,128)S(1)} %cholesky.132), custom_call_target="Cholesky" | custom-call | tf_op jit(solution)/shard_map/jit(cholesky)/cholesky | solution.py:26
  75.9 19.7 %custom-call.18 = f32[1,2,1,128,128]{3,4,2,1,0:T(8,128)S(1)} custom-call(f32[1,2,1,128,128]{4,3,2,1,0:T(8,128)S(1)} %get-tuple-element.26), custom_call_target="InvertDiagBlocksLowerTriangular" | custom-call | tf_op jit(solution)/shard_map/jit(cholesky)/cholesky | solution.py:26
  95.6 0.0 copy-start
  95.6 0.2 bitcast_dynamic-update-slice_fusion
  95.9 0.2 fusion.13
  96.1 11.7 %custom-call.19 = f32[1,2,64,64]{3,2,1,0:T(8,128)S(1)} custom-call(f32[1,2,64,64]{3,2,1,0:T(8,128)S(1)} %fusion.13), custom_call_target="Cholesky" | custom-call | tf_op jit(solution)/shard_map/jit(cholesky)/cholesky | solution.py:26
  107.9 0.1 compare_reduce_fusion
  108.0 0.1 compare_reduce_fusion.1
  108.1 0.1 bitcast_select_fusion
  108.3 0.1 fusion.18
  108.5 39.5 %custom-call.20 = f32[2,2,128,128]{2,3,1,0:T(8,128)S(1)} custom-call(f32[2,2,128,128]{3,2,1,0:T(8,128)S(1)} %pad_maximum_fusion), custom_call_target="InvertDiagBlocksLowerTriangular" | custom-call | tf_op jit(solution)/shard_map/jit(_solve_triangular)/vmap()/triangular_solve | solution.py:27
  148.0 0.0 copy-done
  148.0 0.1 compare_convert_fusion
  148.1 0.0 copy-start.1
  148.1 1.1 fusion.14
  149.2 0.7 convolution_subtract_fusion
  149.9 0.6 fusion.22
  150.5 0.0 copy-done.1
  150.5 2.0 fusion.9
  152.5 0.0 all-gather.2.cloned.1.call-done
  152.5 1.5 copy.30
  154.0 2.8 %fusion.12 = bf16[1024,256]{1,0:T(8,128)(2,1)} fusion(bf16[2,192,1024]{2,1,0:T(8,128)(2,1)} %fusion.9, bf16[2,1024,256]{2,1,0:T(8,128)(2,1)S(1)} %bitcast.75, f32[2,64,1024]{2,1,0:T(8,128)S(1)} %fusion.22, f32[2,128,1024]{2,1,0:T(8,128)S(1)} %fusion.14, f32[2,192]{1,0:T(2,128)S(1)} %compare_convert_fusion), kind=kOutput, calls=%fused_computation.12 | convolution fusion | flops 404193280 | bytes 3933696 | tf_op jit(solution)/shard_map/rcsi,rcsf->rif/dot_general | solution.py:41
  156.8 0.0 all-reduce.5.cloned.1.call-update
  156.8 73.5 %all-reduce.5.cloned.1.call-done = bf16[1024,256]{1,0:T(8,128)(2,1)} async-done(((bf16[1024,256]{1,0:T(8,128)(2,1)}), bf16[1024,256]{1,0:T(8,128)(2,1)}) %all-reduce.5.cloned.1.call-update) | async-done | bytes 524304 | tf_op jit(solution)/shard_map/psum | solution.py:42
  230.3 1.5 dynamic-slice_convert_fusion
  (14 shorter events, 0.2 us)
Async XLA Ops:
  6.5 146.0 %all-gather.2.cloned.1.call-start = ((), (), s32[]{:S(2)}) async-start(), calls=%async_computation | async-start | bytes 1310720 | tf_op jit(solution)/shard_map/all_gather | solution.py:8
  7.3 223.1 %all-reduce.5.cloned.1.call-start = ((), (), s32[]{:S(2)}) async-start(), calls=%async_computation.1 | async-start | bytes 1048576 | tf_op jit(solution)/shard_map/psum | solution.py:42
  95.6 52.4 %copy-start = (s32[1,2]{1,0:T(1,128)S(1)}, s32[1,2]{1,0:T(1,128)}, u32[]{:S(2)}) copy-start(s32[1,2]{1,0:T(1,128)} %param.7) | copy-start | bytes 28
  148.1 2.4 %copy-start.1 = (bf16[1024,2048]{1,0:T(8,128)(2,1)S(1)}, bf16[1024,2048]{1,0:T(8,128)(2,1)}, u32[]{:S(2)}) copy-start(bf16[1024,2048]{1,0:T(8,128)(2,1)} %param.4) | copy-start | bytes 12582916
Sparse Core Ops, SparseCore 0:
  8.9 19.4 all-gather.1
  156.9 73.3 all-reduce.4
where the time goes:
time: 239 us
  other arithmetic  96.8 us (41%)
  waiting for transfers between devices  74.2 us (31%)
  blocking collectives  39 us (16%)
  between operations  13.6 us (6%)
  matrix products  13 us (5%)
    psum x1, waiting for transfers between devices, on_device(): lax.psum(summed.reshape(tile_rows * width, frame_count).astype(jnp.bfloat...  73.5 us
    another operation x10, other arithmetic, on_device(): chol = jnp.linalg.cholesky(gram)  55.4 us
    another operation x7, other arithmetic, on_device(): jax.scipy.linalg.solve_triangular(chol, jnp.swapaxes(sketch, 2, 3), lower...  39.8 us
    all_gather x1, blocking collectives, on_device(): row_block = lax.all_gather(test_matrix, 'tcol', axis=0, tiled=True)  32.5 us
    all_gather x1, blocking collectives, on_device(): lax.all_gather(row_block, 'trow', axis=0, tiled=True)  6.49 us
  transfers between devices with their start and end apart: 2, of which 1 were waited for; matrix products, arithmetic and copies ran while one was open for 44% of the time, Pallas kernels for 0%

commit v1 on v0

--- a/solution.py
+++ b/solution.py
@@ -16,12 +16,37 @@
     sketch_width = test_matrix.shape[1]
     tiles = response.reshape(tile_rows, width, tile_cols, width)
     row_block = lax.all_gather(test_matrix, "tcol", axis=0, tiled=True)
+    tile_out, oldest, t_next = (lax.axis_size("trow"), lax.axis_index("trow"), row_block.shape[0])
+    steps_seen = [(it, (it + 1) % tile_out) for it in range(tile_out)]
+    built = tile_out // 2
+    copies = [(it, (it - 1) % tile_out) for it in range(tile_out)]
     sketch = jnp.einsum(
         "rick,kj->rcij",
-        tiles,
-        lax.all_gather(row_block, "trow", axis=0, tiled=True),
+        lax.dynamic_slice_in_dim(tiles, oldest * t_next, row_block.shape[0], axis=3),
+        row_block,
         preferred_element_type=jnp.float32,
     )
+    raw_out = top = row_block
+    for ii in range(1, built + 1):
+        raw_out = lax.ppermute(raw_out, "trow", steps_seen)
+        if ii < tile_out - built:
+            top = lax.ppermute(top, "trow", copies)
+            sketch = sketch + jnp.einsum(
+                "rick,kj->rcij",
+                lax.dynamic_slice_in_dim(
+                    tiles, (oldest + ii) % tile_out * t_next, top.shape[0], axis=3
+                ),
+                top,
+                preferred_element_type=jnp.float32,
+            )
+        sketch = sketch + jnp.einsum(
+            "rick,kj->rcij",
+            lax.dynamic_slice_in_dim(
+                tiles, (oldest - ii) % tile_out * t_next, raw_out.shape[0], axis=3
+            ),
+            raw_out,
+            preferred_element_type=jnp.float32,
+        )
     gram = jnp.einsum("rcik,rcil->rckl", sketch, sketch, precision=highest)
     chol = jnp.linalg.cholesky(gram)
     basis = jax.scipy.linalg.solve_triangular(chol, jnp.swapaxes(sketch, 2, 3), lower=True)

time: 239 us -> 249 us (1.042)
  local copies, waits for them, and re-layouts: 1.83 us -> 14.2 us
  blocking collectives: 39 us -> 32.5 us
  waiting for transfers between devices: 74.2 us -> 77.2 us
    reshape x0 -> x2, local copies, waits for them, and re-layouts: none -> 9.27 us  [the longest x1 7.8 us: on_device(): tiles = response.reshape(tile_rows, width, tile_cols, width)]
    all_gather x1 -> x0, blocking collectives: 6.49 us -> none  [on_device(): lax.all_gather(row_block, 'trow', axis=0, tiled=True)]
    dynamic_slice x0 -> x1, local copies, waits for them, and re-layouts: none -> 4.58 us  [on_device(): lax.dynamic_slice_in_dim(tiles, (oldest - ii) % tile_out * t_next, raw_ou...]
    ppermute x0 -> x3, waiting for transfers between devices: none -> 3.36 us  [the longest x2 3.36 us: on_device(): raw_out = lax.ppermute(raw_out, 'trow', steps_seen)]
  transfers between devices with their start and end apart: 2 -> 5, of which waited for: 1 -> 2; matrix products, arithmetic and copies ran while one was open for 44% -> 47% of each run, Pallas kernels for 0% -> 0%
where the time goes in v1:
time: 249 us; the launch traced here: 248 us
  other arithmetic  96.8 us (39%)
  waiting for transfers between devices  77.2 us (31%)
  blocking collectives  32.5 us (13%)
  local copies, waits for them, and re-layouts  14.2 us (6%)
  between operations  13.7 us (6%)
  matrix products  12.1 us (5%)
    psum x1, waiting for transfers between devices, on_device(): lax.psum(summed.reshape(tile_rows * width, frame_count).astype(jnp.bfloat...  73.8 us
    another operation x10, other arithmetic, on_device(): chol = jnp.linalg.cholesky(gram)  55.4 us
    another operation x7, other arithmetic, on_device(): jax.scipy.linalg.solve_triangular(chol, jnp.swapaxes(sketch, 2, 3), lower...  39.8 us
    all_gather x1, blocking collectives, on_device(): row_block = lax.all_gather(test_matrix, 'tcol', axis=0, tiled=True)  32.5 us
    reshape x1, local copies, waits for them, and re-layouts, on_device(): tiles = response.reshape(tile_rows, width, tile_cols, width)  7.8 us
  transfers between devices with their start and end apart: 5, of which 2 were waited for; matrix products, arithmetic and copies ran while one was open for 47% of the time, Pallas kernels for 0%

profile of v1, /device:TPU:0, one launch (start us, length us, event | category | flops | bytes accessed | tf_op | source)
XLA Modules:
  0.0 248.5 jit_solution(6105250592057757985)
XLA Ops:
  6.5 0.0 all-gather.2.cloned.1.call-start
  6.5 32.5 %all_gather.6 = bf16[256,192]{1,0:T(8,128)(2,1)S(1)} all-gather(bf16[32,192]{1,0:T(8,128)(2,1)} %param.5), channel_id=1, replica_groups=mesh['trow'=4,'tcol'=8] {'tcol'}, dimensions={0}, use_global_device_ids=true | all-gather | bytes 110592 | tf_op jit(solution)/shard_map/all_gather | solution.py:18
  39.1 0.0 collective-permute-start.1
  39.1 1.7 collective-permute-start
  40.8 0.0 all-gather.2.cloned.1.call-update
  40.8 0.0 all-reduce.5.cloned.1.call-start
  41.0 7.8 %reshape.154 = bf16[1,1024,2,1024]{3,2,1,0:T(2,128)(2,1)} reshape(bf16[1024,2048]{1,0:T(8,128)(2,1)} %param.4) | data formatting | bytes 8388608 | tf_op jit(solution)/shard_map/reshape | solution.py:17
  48.8 4.6 %constant_dynamic-slice_fusion = (bf16[1,1024,2,256]{3,2,1,0:T(2,128)(2,1)S(1)}, bf16[1,1024,2,256]{3,2,1,0:T(2,128)(2,1)S(1)}, bf16[1,1024,2,256]{3,2,1,0:T(2,128)(2,1)S(1)}, bf16[1,1024,2,256]{3,2,1,0:T(2,128)(2,1)S(1)}) fusion(bf16[1,1024,2,1024]{3,2,1,0:T(2,128)(2,1)} %reshape.154, s32[]{:T(128)S(6)} %select_n.40, s32[]{:T(128)S(6)} %select_n.38, ...), kind=kLoop, calls=%fused_computation.59 | loop fusion | bytes 8388624 | tf_op jit(solution)/shard_map/dynamic_slice | solution.py:44
  53.4 0.0 copy-start.2
  53.4 0.5 fusion.15
  53.9 0.1 copy-done.2
  54.1 0.1 compare_convert_fusion
  54.2 0.0 collective-permute-done.1
  54.2 0.1 collective-permute-start.2
  54.2 0.5 fusion.13
  54.7 0.0 collective-permute-done
  54.7 0.5 fusion.14
  55.3 3.4 %collective-permute-done.2 = bf16[256,192]{1,0:T(8,128)(2,1)S(1)} collective-permute-done((bf16[256,192]{1,0:T(8,128)(2,1)S(1)}, bf16[256,192]{1,0:T(8,128)(2,1)S(1)}, u32[]{:S(2)}, u32[]{:S(2)}) %collective-permute-start.2) | collective-permute-done | bytes 98336 | tf_op jit(solution)/shard_map/ppermute | solution.py:31
  58.6 0.5 add_add_fusion
  59.1 1.7 fusion.4
  60.8 0.2 copy.26
  61.0 0.1 fusion.17
  61.1 23.6 %custom-call.17 = f32[1,2,128,128]{3,2,1,0:T(8,128)S(1)} custom-call(f32[1,2,128,128]{3,2,1,0:T(8,128)S(1)} %cholesky.132), custom_call_target="Cholesky" | custom-call | tf_op jit(solution)/shard_map/jit(cholesky)/cholesky | solution.py:51
  84.8 19.7 %custom-call.18 = f32[1,2,1,128,128]{3,4,2,1,0:T(8,128)S(1)} custom-call(f32[1,2,1,128,128]{4,3,2,1,0:T(8,128)S(1)} %get-tuple-element.30), custom_call_target="InvertDiagBlocksLowerTriangular" | custom-call | tf_op jit(solution)/shard_map/jit(cholesky)/cholesky | solution.py:51
  104.5 0.2 bitcast_dynamic-update-slice_fusion
  104.7 0.2 fusion.10
  105.0 11.7 %custom-call.19 = f32[1,2,64,64]{3,2,1,0:T(8,128)S(1)} custom-call(f32[1,2,64,64]{3,2,1,0:T(8,128)S(1)} %fusion.10), custom_call_target="Cholesky" | custom-call | tf_op jit(solution)/shard_map/jit(cholesky)/cholesky | solution.py:51
  116.7 0.1 compare_reduce_fusion
  116.8 0.1 compare_reduce_fusion.1
  117.0 0.1 bitcast_select_fusion
  117.1 0.1 fusion.18
  117.3 39.5 %custom-call.20 = f32[2,2,128,128]{2,3,1,0:T(8,128)S(1)} custom-call(f32[2,2,128,128]{3,2,1,0:T(8,128)S(1)} %pad_maximum_fusion), custom_call_target="InvertDiagBlocksLowerTriangular" | custom-call | tf_op jit(solution)/shard_map/jit(_solve_triangular)/vmap()/triangular_solve | solution.py:52
  156.8 0.0 copy-start.1
  156.8 0.0 copy-start
  156.9 1.1 fusion.11
  157.9 0.0 copy-done.1
  157.9 0.7 fusion.25
  158.6 1.5 fusion.16
  160.1 0.0 copy-done
  160.2 1.9 fusion.6
  162.1 0.0 all-gather.2.cloned.1.call-done
  162.1 1.5 copy.43
  163.6 2.8 %fusion.9 = bf16[1024,256]{1,0:T(8,128)(2,1)} fusion(bf16[2,192,1024]{2,1,0:T(8,128)(2,1)} %fusion.6, bf16[2,1024,256]{2,1,0:T(8,128)(2,1)S(1)} %bitcast.96, f32[2,64,1024]{2,1,0:T(8,128)S(1)} %fusion.16, f32[2,128,1024]{2,1,0:T(8,128)S(1)} %fusion.11, f32[2,192]{1,0:T(2,128)S(1)} %compare_convert_fusion), kind=kOutput, calls=%fused_computation.10 | convolution fusion | flops 404193280 | bytes 3933696 | tf_op jit(solution)/shard_map/rcsi,rcsf->rif/dot_general | solution.py:66
  166.3 0.0 all-reduce.5.cloned.1.call-update
  166.3 73.8 %all-reduce.5.cloned.1.call-done = bf16[1024,256]{1,0:T(8,128)(2,1)} async-done(((bf16[1024,256]{1,0:T(8,128)(2,1)}), bf16[1024,256]{1,0:T(8,128)(2,1)}) %all-reduce.5.cloned.1.call-update) | async-done | bytes 524304 | tf_op jit(solution)/shard_map/psum | solution.py:67
  240.1 1.5 dynamic-slice_convert_fusion
  (14 shorter events, 0.2 us)
Async XLA Ops:
  6.5 155.6 %all-gather.2.cloned.1.call-start = ((), (), s32[]{:S(2)}) async-start(), calls=%async_computation | async-start | bytes 1310720 | tf_op jit(solution)/shard_map/all_gather | solution.py:8
  39.1 15.1 %collective-permute-start.1 = (bf16[256,192]{1,0:T(8,128)(2,1)S(1)}, bf16[256,192]{1,0:T(8,128)(2,1)S(1)}, u32[]{:S(2)}, u32[]{:S(2)}) collective-permute-start(bf16[256,192]{1,0:T(8,128)(2,1)S(1)} %all_gather.6), channel_id=1, source_target_pairs={{0,8},{8,16},{16,24},{24,0},{1,9},{9,17},{17,25},{25,1},{2,10},{10... | collective-permute-start | bytes 294920 | tf_op jit(solution)/shard_map/ppermute | solution.py:31
  39.1 15.7 %collective-permute-start = (bf16[256,192]{1,0:T(8,128)(2,1)S(1)}, bf16[256,192]{1,0:T(8,128)(2,1)S(1)}, u32[]{:S(2)}, u32[]{:S(2)}) collective-permute-start(bf16[256,192]{1,0:T(8,128)(2,1)S(1)} %all_gather.6), channel_id=1, source_target_pairs={{0,24},{8,0},{16,8},{24,16},{1,25},{9,1},{17,9},{25,17},{2,26},{10... | collective-permute-start | bytes 294920 | tf_op jit(solution)/shard_map/ppermute | solution.py:33
  40.8 199.3 %all-reduce.5.cloned.1.call-start = ((), (), s32[]{:S(2)}) async-start(), calls=%async_computation.1 | async-start | bytes 1048576 | tf_op jit(solution)/shard_map/psum | solution.py:67
  53.4 0.7 copy-start.2
  54.2 4.4 %collective-permute-start.2 = (bf16[256,192]{1,0:T(8,128)(2,1)S(1)}, bf16[256,192]{1,0:T(8,128)(2,1)S(1)}, u32[]{:S(2)}, u32[]{:S(2)}) collective-permute-start(bf16[256,192]{1,0:T(8,128)(2,1)S(1)} %collective-permute-done.1), channel_id=1, source_target_pairs={{0,8},{8,16},{16,24},{24,0},{1,9},{9,17},{17,25},{25,1},{2,10},{10... | collective-permute-start | bytes 294920 | tf_op jit(solution)/shard_map/ppermute | solution.py:31
  156.8 1.1 copy-start.1
  156.8 3.3 %copy-start = (bf16[1024,2048]{1,0:T(8,128)(2,1)S(1)}, bf16[1024,2048]{1,0:T(8,128)(2,1)}, u32[]{:S(2)}) copy-start(bf16[1024,2048]{1,0:T(8,128)(2,1)} %param.4) | copy-start | bytes 12582916
Sparse Core Ops, SparseCore 0:
  41.0 17.5 all-gather.1
  166.5 73.5 all-reduce.4
